TPU v7x, 32 devices: a whole 2x2x4 slice. The times are simulated.
32 devices in a mesh: pipe: 4 (over z), expert: 8 (over y, x, core).
Axes of the slice: x: 2, y: 2, z: 4, core: 2. Of those that a mesh axis runs over, the one named last changes fastest.
Arguments:
- acts: bfloat16 [4, 64, 3584], P('pipe', 'expert'), may hold values from -6 to 6
- grads: bfloat16 [4, 64, 3584], P('pipe', 'expert'), may hold values from -6 to 6
- norm_gain: float32 [4, 3584], P('pipe'), may hold values from 0.1 to 1.9
- router: float32 [4, 3584, 8], P('pipe'), may hold values from -0.09375 to 0.09375
- w_gate: bfloat16 [4, 3584, 8192], P('pipe', None, 'expert'), may hold values from -0.09375 to 0.09375
- w_up: bfloat16 [4, 3584, 8192], P('pipe', None, 'expert'), may hold values from -0.09375 to 0.09375
- w_down: bfloat16 [4, 8192, 3584], P('pipe', 'expert'), may hold values from -0.1875 to 0.1875
- expert_ids: int32 [4, 64, 2], P('pipe', 'expert'), may hold values from 0 to 7, all different within a row; in each aligned block of 8 rows (0 to 7, 8 to 15, ..., all dimensions but the last counted through in order) at most 4 rows name the same one
Outputs:
- arrived: bfloat16 [4, 64, 3584], P('pipe', 'expert')
- returned: bfloat16 [4, 64, 3584], P('pipe', 'expert')
Inputs may be any that keep to these rules, and one draw needn't show every extreme that they name: `expert_ids`: A token's 2 experts differ. Within the tokens of one device (aligned blocks of 8 tokens of one section), no expert is chosen more than 4 times, and some block chooses some expert exactly 4 times.
All inputs are finite; a program needn't handle non-finite values.
Results may differ from a plain program's by a relative error of at most 0.0058.
Values may be sent and summed in bfloat16 or wider, within the bound.
No kernel may reach another device: no remote copies, remote signals or barrier semaphores. Data moves between devices by JAX's collectives and lax.ppermute only.
A program may use at most 64 MiB of HBM per device.

v0:
```python
import functools
import jax
import jax.numpy as jnp
from jax import lax
from jax.experimental import pallas as pl
from jax.experimental.pallas import tpu as pltpu
from jax.sharding import PartitionSpec as P

EXPERTS = 8
LANES = 128
EPS = 1e-06
F32 = jnp.float32
BF16 = jnp.bfloat16


VMEM = pl.BlockSpec(memory_space=pltpu.VMEM)
HBM = pl.BlockSpec(memory_space=pltpu.HBM)
SMEM = pl.BlockSpec(memory_space=pltpu.SMEM)


def flip(value, bit):
    count = lax.axis_size("expert")
    return lax.ppermute(value, "expert", [(i, i ^ bit) for i in range(count)])


def pack_kernel(x_hbm, g_hbm, ids_hbm, o_ref, ids_ref, sems):
    rows, width = x_hbm.shape
    copies = [
        pltpu.make_async_copy(ids_hbm, ids_ref, sems.at[0]),
        pltpu.make_async_copy(x_hbm, o_ref.at[0, pl.ds(0, rows), pl.ds(0, width)], sems.at[1]),
        pltpu.make_async_copy(g_hbm, o_ref.at[0, pl.ds(rows, rows), pl.ds(0, width)], sems.at[2]),
    ]
    for copy in copies:
        copy.start()
    o_ref[0, rows:, width:] = jnp.zeros((rows, LANES), BF16)
    lane = lax.broadcasted_iota(jnp.int32, (rows, LANES), 1)
    across = lax.broadcasted_iota(jnp.int32, (rows, rows), 1)
    down = lax.broadcasted_iota(jnp.int32, (rows, rows), 0)
    copies[0].wait()
    ids = ids_ref[...].astype(F32)
    tail = jnp.zeros((rows, LANES), F32)
    for k in range(ids.shape[0]):
        column = jnp.sum(jnp.where(across == down, ids[k : k + 1, :], 0.0), axis=1, keepdims=True)
        tail = jnp.where(lane == k, column, tail)
    o_ref[0, :rows, width:] = tail.astype(BF16)
    copies[1].wait()
    copies[2].wait()


def pack(x, g, ids):
    rows, width = x.shape
    return pl.pallas_call(
        pack_kernel,
        out_shape=pltpu.VMEM((1, 2 * rows, width + LANES), BF16),
        in_specs=[HBM] * 3,
        out_specs=VMEM,
        scratch_shapes=[pltpu.VMEM(ids.shape, jnp.int32), pltpu.SemaphoreType.DMA((3,))],
        name="pack",
        compiler_params=pltpu.CompilerParams(vmem_limit_bytes=1 << 20),
        cost_estimate=pl.CostEstimate(flops=0, bytes_accessed=8 * rows * width, transcendentals=0),
    )(*[pltpu.with_memory_space_constraint(a, pltpu.HBM) for a in (x, g, ids)])


def fetch_kernel(*refs):
    count = (len(refs) - 3) // 2
    sources, targets, sems = refs[:count], refs[count + 2 : -1], refs[-1]
    copies = [pltpu.make_async_copy(a, b, sems.at[i]) for i, (a, b) in enumerate(zip(sources, targets))]
    for copy in copies:
        copy.start()
    for copy in copies:
        copy.wait()


def fetch(after, me, *arrays):
    count = len(arrays)
    held = sum(a.size * a.dtype.itemsize for a in arrays)
    return pl.pallas_call(
        fetch_kernel,
        out_shape=[pltpu.VMEM(a.shape, a.dtype) for a in arrays],
        in_specs=[HBM] * count + [pl.BlockSpec(memory_space=pl.ANY), SMEM],
        out_specs=[VMEM] * count,
        scratch_shapes=[pltpu.SemaphoreType.DMA((count,))],
        name="fetch",
        compiler_params=pltpu.CompilerParams(vmem_limit_bytes=1 << 20),
        cost_estimate=pl.CostEstimate(flops=0, bytes_accessed=held, transcendentals=0),
    )(*[pltpu.with_memory_space_constraint(a, pltpu.HBM) for a in arrays], after, me)


def contract_last(left, right):
    return lax.dot_general(left, right, (((1,), (1,)), ((), ())), preferred_element_type=F32)


def thirds(value):
    high = value.astype(BF16)
    rest = value - high.astype(F32)
    middle = rest.astype(BF16)
    return high, middle, (rest - middle.astype(F32)).astype(BF16)


def expert_kernel(top, me_ref, gain_ref, router_ref, wg_ref, wu_ref, wd_hbm, *refs):
    pieces, outs = refs[:8], refs[8:16]
    nb, sg, gate_s, up_s, out_s, hid_s, dg_s, du_s, route_s, wd_ref, wd_sem = refs[16:]
    wd_copy = pltpu.make_async_copy(wd_hbm, wd_ref, wd_sem)
    wd_copy.start()
    blocks, double, _ = pieces[0].shape
    rows = double // 2
    width, units = wg_ref.shape
    step_f = units
    step_d = width
    mine = me_ref[0]
    gain = gain_ref[...]
    router = router_ref[...]
    r_hi, r_mid, r_lo = thirds(router)
    split = jnp.concatenate([r_hi, r_mid, r_lo], axis=0)
    route_s[...] = jnp.concatenate([r_hi, r_mid, r_lo, r_hi, r_mid, r_hi], axis=0)
    routes = route_s
    total_rows = 8 * rows
    lane = lax.broadcasted_iota(jnp.int32, (total_rows, EXPERTS), 1)

    def block(h, carry):
        x = jnp.concatenate([p[h, :rows, :width].astype(F32) for p in pieces], axis=0)
        dy = jnp.concatenate([p[h, rows:, :width].astype(F32) for p in pieces], axis=0)
        ids = jnp.concatenate([p[h, :rows, width:].astype(F32) for p in pieces], axis=0)
        inv = lax.rsqrt(jnp.mean(x * x, axis=-1, keepdims=True) + EPS)
        nb[...] = (x * inv * gain).astype(BF16)
        parts = contract_last(nb[...], split)
        logits = parts[:, :EXPERTS] + parts[:, EXPERTS : 2 * EXPERTS] + parts[:, 2 * EXPERTS :]
        affinity = 1.0 / (1.0 + jnp.exp(-logits))
        chosen = jnp.zeros((total_rows, EXPERTS), F32)
        for k in range(top):
            chosen += (ids[:, k : k + 1].astype(jnp.int32) == lane).astype(F32)
        total = jnp.sum(chosen * affinity, axis=-1, keepdims=True)
        here = chosen * (lane == mine).astype(F32)
        has = jnp.sum(here, axis=-1, keepdims=True)
        weight = jnp.sum(here * affinity, axis=-1, keepdims=True) / total
        sg[...] = (weight * dy).astype(BF16)

        def first(n, c):
            cols = pl.ds(n * step_f, step_f)
            gate_s[:, cols] = jnp.dot(nb[...], wg_ref[:, cols], preferred_element_type=F32)
            up_s[:, cols] = jnp.dot(nb[...], wu_ref[:, cols], preferred_element_type=F32)
            return c

        for n in range(units // step_f):
            first(n, 0)
        gate = gate_s[...]
        up = up_s[...]
        sigma = 1.0 / (1.0 + jnp.exp(-gate))
        active = gate * sigma
        slope = sigma * (1.0 + gate * (1.0 - sigma))
        hid_s[...] = (active * up).astype(BF16)

        if blocks == 1:
            wd_copy.wait()

        def second(n, c):
            cols = pl.ds(n * step_d, step_d)
            out_s[:, cols] = jnp.dot(hid_s[...], wd_ref[:, cols], preferred_element_type=F32)
            return c

        for n in range(width // step_d):
            second(n, 0)
        out = out_s[...]
        dweight = has * jnp.sum(dy * out, axis=-1, keepdims=True)
        share = (weight * out).astype(BF16)
        for q in range(8):
            outs[q][h, :rows, :] = share[q * rows : (q + 1) * rows]
        coef = chosen * affinity * (1.0 - affinity) * ((lane == mine).astype(F32) - weight)
        coef = coef * (dweight / total)
        c_hi, c_mid, c_lo = thirds(coef)
        coefs = jnp.concatenate([c_hi, c_hi, c_hi, c_mid, c_mid, c_lo], axis=1)

        def third(n, c):
            cols = pl.ds(n * step_f, step_f)
            gate_s[:, cols] = contract_last(sg[...], wd_ref[cols, :])
            return c

        for n in range(units // step_f):
            third(n, 0)
        dhidden = gate_s[...]
        dg_s[...] = (dhidden * up * slope).astype(BF16)
        du_s[...] = (dhidden * active).astype(BF16)

        def fourth(n, c):
            cols = pl.ds(n * step_d, step_d)
            out_s[:, cols] = (
                contract_last(dg_s[...], wg_ref[cols, :])
                + contract_last(du_s[...], wu_ref[cols, :])
                + jnp.dot(coefs, routes[:, cols], preferred_element_type=F32)
            )
            return c

        for n in range(width // step_d):
            fourth(n, 0)
        u = out_s[...] * gain
        x = jnp.concatenate([p[h, :rows, :width].astype(F32) for p in pieces], axis=0)
        m = jnp.mean(u * x, axis=-1, keepdims=True)
        din = (inv * u - x * (inv * inv * inv * m)).astype(BF16)
        for q in range(8):
            outs[q][h, rows:, :] = din[q * rows : (q + 1) * rows]
        return carry

    if blocks == 1:
        block(0, 0)
    else:
        wd_copy.wait()
        lax.fori_loop(0, blocks, block, 0)


def experts(top, me, gain, router, wg, wu, wd, pieces):
    blocks, double, _ = pieces[0].shape
    width, units = wg.shape
    total = 8 * double // 2
    return pl.pallas_call(
        functools.partial(expert_kernel, top),
        out_shape=[jax.ShapeDtypeStruct((blocks, double, width), BF16)] * 8,
        in_specs=[SMEM] + [VMEM] * 4 + [HBM] + [VMEM] * 8,
        out_specs=[VMEM] * 8,
        scratch_shapes=[
            pltpu.VMEM((total, width), BF16),
            pltpu.VMEM((total, width), BF16),
            pltpu.VMEM((total, units), F32),
            pltpu.VMEM((total, units), F32),
            pltpu.VMEM((total, width), F32),
            pltpu.VMEM((total, units), BF16),
            pltpu.VMEM((total, units), BF16),
            pltpu.VMEM((total, units), BF16),
            pltpu.VMEM((6 * EXPERTS, width), BF16),
            pltpu.VMEM((units, width), BF16),
            pltpu.SemaphoreType.DMA,
        ],
        compiler_params=pltpu.CompilerParams(vmem_limit_bytes=VMEM_LIMIT),
        name="experts",
    )(me, gain, router, wg, wu, wd, *pieces)


VMEM_LIMIT = 24 << 20


def add(a, b):
    return (a.astype(F32) + b.astype(F32)).astype(BF16)


def section_step(acts, grads, norm_gain, router, w_gate, w_up, w_down, expert_ids):
    x, dy, ids = acts[0], grads[0], expert_ids[0]
    rows, _ = x.shape
    count = lax.axis_size("expert")
    groups = count // EXPERTS
    me = (lax.axis_index("expert") // groups).astype(jnp.int32).reshape(1)
    own = pack(x, dy, ids.T)
    bit = 8
    while bit < count:
        own = jnp.concatenate([own, flip(own, bit)], axis=0)
        bit *= 2
    wg, wu, route, gain = fetch(own, me, w_gate[0], w_up[0], router[0].T, norm_gain)
    pieces = {0: own}
    for j in (6, 2, 4):
        pieces[j] = flip(own, j)
    for j in (0, 2, 4, 6):
        pieces[j + 1] = flip(pieces[j], 1)
    outs = experts(
        ids.shape[1], me, gain, route, wg, wu, pltpu.with_memory_space_constraint(w_down[0], pltpu.HBM),
        [pieces[j] for j in range(8)],
    )
    kept = {j: add(outs[j], flip(outs[j + 1], 1)) for j in (6, 2, 4, 0)}
    came = [flip(kept[j], j) for j in (6, 2, 4)]
    if count > 8:
        got = kept[0].astype(F32) + sum(c.astype(F32) for c in came)
        bit = count // 2
        while bit >= 8:
            half = got.shape[0] // 2
            got = got[:half] + flip(got[half:].astype(BF16), bit).astype(F32)
            bit //= 2
    else:
        got = kept[0].astype(F32) + sum(c.astype(F32) for c in came)
    section_out = (x.astype(F32) + got[0, :rows]).astype(BF16)
    section_grad = (dy.astype(F32) + got[0, rows:]).astype(BF16)
    stages = lax.axis_size("pipe")
    odd = lax.axis_index("pipe") % 2 == 1
    first = jnp.where(odd, section_grad, section_out)
    second = jnp.where(odd, section_out, section_grad)

    def trade(value, parity):
        pairs = []
        for s in range(parity, stages - 1, 2):
            pairs += [(s, s + 1), (s + 1, s)]
        return lax.ppermute(value, "pipe", pairs)

    first = trade(first, 0)
    second = trade(second, 1)
    arrived = jnp.where(odd, first, second)
    returned = jnp.where(odd, second, first)
    return (arrived[None], returned[None])


def solution(mesh):
    return jax.shard_map(
        section_step,
        mesh=mesh,
        in_specs=(
            P("pipe", "expert", None),
            P("pipe", "expert", None),
            P("pipe", None),
            P("pipe", None, None),
            P("pipe", None, "expert"),
            P("pipe", None, "expert"),
            P("pipe", "expert", None),
            P("pipe", "expert", None),
        ),
        out_specs=(P("pipe", "expert", None), P("pipe", "expert", None)),
        check_vma=False,
    )
```

profile of v0, /device:TPU:0, one launch (start us, length us, event | category | flops | bytes accessed | tf_op | source)
XLA Modules:
  0.0 47.1 jit_solution(9477568518169149168)
XLA Ops:
  0.6 0.9 %pack.1.refs_4_.refs_0_ = bf16[1,16,3712]{2,1,0:T(8,128)(2,1)S(1)} custom-call(bf16[8,3584]{1,0:T(8,128)(2,1)} %bitcast.49, bf16[8,3584]{1,0:T(8,128)(2,1)} %bitcast.50, s32[2,8]{1,0:T(2,128)} %bitcast.52), custom_call_target="tpu_custom_call" | custom-call | bytes 229376 | tf_op jit(solution)/shard_map/pack/pallas_call | solution.py:52
  1.5 4.0 %collective-permute-start.5 = (bf16[1,16,3712]{2,1,0:T(8,128)(2,1)S(1)}, bf16[1,16,3712]{2,1,0:T(8,128)(2,1)S(1)}, u32[]{:S(2)}, u32[]{:S(2)}) collective-permute-start(bf16[1,16,3712]{2,1,0:T(8,128)(2,1)S(1)} %pack.1.refs_4_.refs_0_), channel_id=1, source_target_pairs={{0,6},{1,7},{2,4},{3,5},{4,2},{5,3},{6,0},{7,1},{8,14},{9,15},{10,... | collective-permute-start | bytes 356360 | tf_op jit(solution)/shard_map/ppermute | solution.py:23
  5.5 0.5 %collective-permute-start.3 = (bf16[1,16,3712]{2,1,0:T(8,128)(2,1)S(1)}, bf16[1,16,3712]{2,1,0:T(8,128)(2,1)S(1)}, u32[]{:S(2)}, u32[]{:S(2)}) collective-permute-start(bf16[1,16,3712]{2,1,0:T(8,128)(2,1)S(1)} %pack.1.refs_4_.refs_0_), channel_id=1, source_target_pairs={{0,4},{1,5},{2,6},{3,7},{4,0},{5,1},{6,2},{7,3},{8,12},{9,13},{10,... | collective-permute-start | bytes 356360 | tf_op jit(solution)/shard_map/ppermute | solution.py:23
  6.0 0.1 collective-permute-start.1
  6.2 0.0 collective-permute-start
  6.2 3.0 %collective-permute-done.5.refs_6_ = bf16[1,16,3712]{2,1,0:T(8,128)(2,1)S(1)} collective-permute-done((bf16[1,16,3712]{2,1,0:T(8,128)(2,1)S(1)}, bf16[1,16,3712]{2,1,0:T(8,128)(2,1)S(1)}, u32[]{:S(2)}, u32[]{:S(2)}) %collective-permute-start.5) | collective-permute-done | bytes 118816 | tf_op jit(solution)/shard_map/ppermute | solution.py:23
  9.1 0.0 collective-permute-start.6
  9.1 2.2 %collective-permute-done.3.refs_4_ = bf16[1,16,3712]{2,1,0:T(8,128)(2,1)S(1)} collective-permute-done((bf16[1,16,3712]{2,1,0:T(8,128)(2,1)S(1)}, bf16[1,16,3712]{2,1,0:T(8,128)(2,1)S(1)}, u32[]{:S(2)}, u32[]{:S(2)}) %collective-permute-start.3) | collective-permute-done | bytes 118816 | tf_op jit(solution)/shard_map/ppermute | solution.py:23
  11.3 0.0 collective-permute-start.4
  11.3 0.2 collective-permute-done.1.refs_2_
  11.5 0.3 collective-permute-start.2
  11.8 5.2 %fetch.1 = (bf16[3584,1024]{1,0:T(8,128)(2,1)S(1)}, bf16[3584,1024]{1,0:T(8,128)(2,1)S(1)}, f32[8,3584]{1,0:T(8,128)S(1)}, f32[1,3584]{1,0:T(1,128)S(1)}) custom-call(bf16[3584,1024]{1,0:T(8,128)(2,1)} %bitcast.46, bf16[3584,1024]{1,0:T(8,128)(2,1)} %bitcast.47, f32[8,3584]{1,0:T(8,128)} %bitcast.51, f32[1,3584]{1,0:T(1,128)} %refs_3_.1, ...), custom_call_target="tpu_custom_call" | custom-call | bytes 14809088 | tf_op jit(solution)/shard_map/fetch/pallas_call | solution.py:77
  17.0 0.0 collective-permute-done.refs_1_
  17.0 0.0 collective-permute-done.6.refs_7_
  17.0 0.0 collective-permute-done.4.refs_5_
  17.1 0.0 collective-permute-done.2.refs_3_
  17.1 0.0 copy-start
  17.1 0.0 copy-start.1
  17.1 11.6 %experts.1 = (bf16[1,16,3584]{2,1,0:T(8,128)(2,1)S(1)}, bf16[1,16,3584]{2,1,0:T(8,128)(2,1)S(1)}, bf16[1,16,3584]{2,1,0:T(8,128)(2,1)S(1)}, bf16[1,16,3584]{2,1,...) custom-call(s32[1]{0:T(128)} %bitcast.1.refs_5_.me_ref, ...), custom_call_target="tpu_custom_call" | custom-call | tf_op jit(solution)/shard_map/experts/pallas_call | solution.py:214
  28.7 0.3 collective-permute-start.8
  29.1 0.3 collective-permute-start.7
  29.3 0.2 collective-permute-start.10
  29.6 0.3 collective-permute-start.12
  29.8 0.3 collective-permute-done.8
  30.2 1.9 %collective-permute-start.9 = (bf16[1,16,3584]{2,1,0:T(8,128)(2,1)S(1)}, bf16[1,16,3584]{2,1,0:T(8,128)(2,1)S(1)}, u32[]{:S(2)}, u32[]{:S(2)}) collective-permute-start(bf16[1,16,3584]{2,1,0:T(8,128)(2,1)S(1)} %add_convert_fusion.2), channel_id=1, source_target_pairs={{0,6},{1,7},{2,4},{3,5},{4,2},{5,3},{6,0},{7,1},{8,14},{9,15},{10,... | collective-permute-start | bytes 344072 | tf_op jit(solution)/shard_map/ppermute | solution.py:23
  32.1 0.0 collective-permute-done.10
  32.1 1.4 %collective-permute-start.11 = (bf16[1,16,3584]{2,1,0:T(8,128)(2,1)S(1)}, bf16[1,16,3584]{2,1,0:T(8,128)(2,1)S(1)}, u32[]{:S(2)}, u32[]{:S(2)}) collective-permute-start(bf16[1,16,3584]{2,1,0:T(8,128)(2,1)S(1)} %add_convert_fusion.1), channel_id=1, source_target_pairs={{0,2},{1,3},{2,0},{3,1},{4,6},{5,7},{6,4},{7,5},{8,10},{9,11},{10,... | collective-permute-start | bytes 344072 | tf_op jit(solution)/shard_map/ppermute | solution.py:23
  33.5 0.0 collective-permute-done.12
  33.6 0.4 collective-permute-start.13
  33.9 0.0 collective-permute-done.7
  33.9 3.2 %collective-permute-done.9 = bf16[1,16,3584]{2,1,0:T(8,128)(2,1)S(1)} collective-permute-done((bf16[1,16,3584]{2,1,0:T(8,128)(2,1)S(1)}, bf16[1,16,3584]{2,1,0:T(8,128)(2,1)S(1)}, u32[]{:S(2)}, u32[]{:S(2)}) %collective-permute-start.9) | collective-permute-done | bytes 114720 | tf_op jit(solution)/shard_map/ppermute | solution.py:23
  37.2 1.9 %collective-permute-done.11 = bf16[1,16,3584]{2,1,0:T(8,128)(2,1)S(1)} collective-permute-done((bf16[1,16,3584]{2,1,0:T(8,128)(2,1)S(1)}, bf16[1,16,3584]{2,1,0:T(8,128)(2,1)S(1)}, u32[]{:S(2)}, u32[]{:S(2)}) %collective-permute-start.11) | collective-permute-done | bytes 114720 | tf_op jit(solution)/shard_map/ppermute | solution.py:23
  39.0 0.0 collective-permute-done.13
  39.1 0.1 add_add_fusion
  39.1 0.0 copy-done
  39.1 0.0 copy-done.1
  39.2 0.7 %collective-permute-start.15 = (bf16[8,3584]{1,0:T(8,128)(2,1)S(1)}, bf16[8,3584]{1,0:T(8,128)(2,1)S(1)}, u32[]{:S(2)}, u32[]{:S(2)}) collective-permute-start(bf16[8,3584]{1,0:T(8,128)(2,1)S(1)} %get-tuple-element.26), channel_id=1, source_target_pairs={{8,16},{16,8},{9,17},{17,9},{10,18},{18,10},{11,19},{19,11},{12,20... | collective-permute-start | bytes 172040 | tf_op jit(solution)/shard_map/ppermute | solution.py:287
  39.9 4.5 %collective-permute-start.14 = (bf16[8,3584]{1,0:T(8,128)(2,1)S(1)}, bf16[8,3584]{1,0:T(8,128)(2,1)S(1)}, u32[]{:S(2)}, u32[]{:S(2)}) collective-permute-start(bf16[8,3584]{1,0:T(8,128)(2,1)S(1)} %get-tuple-element.27), channel_id=1, source_target_pairs={{0,8},{8,0},{16,24},{24,16},{1,9},{9,1},{17,25},{25,17},{2,10},{10... | collective-permute-start | bytes 172040 | tf_op jit(solution)/shard_map/ppermute | solution.py:287
  44.3 0.0 collective-permute-done.15
  44.3 2.2 %collective-permute-done.14 = bf16[8,3584]{1,0:T(8,128)(2,1)S(1)} collective-permute-done((bf16[8,3584]{1,0:T(8,128)(2,1)S(1)}, bf16[8,3584]{1,0:T(8,128)(2,1)S(1)}, u32[]{:S(2)}, u32[]{:S(2)}) %collective-permute-start.14) | collective-permute-done | bytes 57376 | tf_op jit(solution)/shard_map/ppermute | solution.py:287
  46.5 0.7 %select_bitcast_fusion = (bf16[1,8,3584]{2,1,0:T(8,128)(2,1)}, bf16[1,8,3584]{2,1,0:T(8,128)(2,1)}) fusion(bf16[8,3584]{1,0:T(8,128)(2,1)S(1)} %collective-permute-done.15, bf16[8,3584]{1,0:T(8,128)(2,1)S(1)} %collective-permute-done.14, pred[]{:T(512)S(6)} %eq.5), kind=kLoop, calls=%fused_computation.11 | loop fusion | flops 57344 | bytes 229377 | tf_op jit(solution)/shard_map/broadcast_in_dim | solution.py:293
  (4 shorter events, 0.1 us)
Async XLA Ops:
  1.5 7.6 %collective-permute-start.5 = (bf16[1,16,3712]{2,1,0:T(8,128)(2,1)S(1)}, bf16[1,16,3712]{2,1,0:T(8,128)(2,1)S(1)}, u32[]{:S(2)}, u32[]{:S(2)}) collective-permute-start(bf16[1,16,3712]{2,1,0:T(8,128)(2,1)S(1)} %pack.1.refs_4_.refs_0_), channel_id=1, source_target_pairs={{0,6},{1,7},{2,4},{3,5},{4,2},{5,3},{6,0},{7,1},{8,14},{9,15},{10,... | collective-permute-start | bytes 356360 | tf_op jit(solution)/shard_map/ppermute | solution.py:23
  5.5 5.8 %collective-permute-start.3 = (bf16[1,16,3712]{2,1,0:T(8,128)(2,1)S(1)}, bf16[1,16,3712]{2,1,0:T(8,128)(2,1)S(1)}, u32[]{:S(2)}, u32[]{:S(2)}) collective-permute-start(bf16[1,16,3712]{2,1,0:T(8,128)(2,1)S(1)} %pack.1.refs_4_.refs_0_), channel_id=1, source_target_pairs={{0,4},{1,5},{2,6},{3,7},{4,0},{5,1},{6,2},{7,3},{8,12},{9,13},{10,... | collective-permute-start | bytes 356360 | tf_op jit(solution)/shard_map/ppermute | solution.py:23
  6.0 5.5 %collective-permute-start.1 = (bf16[1,16,3712]{2,1,0:T(8,128)(2,1)S(1)}, bf16[1,16,3712]{2,1,0:T(8,128)(2,1)S(1)}, u32[]{:S(2)}, u32[]{:S(2)}) collective-permute-start(bf16[1,16,3712]{2,1,0:T(8,128)(2,1)S(1)} %pack.1.refs_4_.refs_0_), channel_id=1, source_target_pairs={{0,2},{1,3},{2,0},{3,1},{4,6},{5,7},{6,4},{7,5},{8,10},{9,11},{10,... | collective-permute-start | bytes 356360 | tf_op jit(solution)/shard_map/ppermute | solution.py:23
  6.2 10.9 %collective-permute-start = (bf16[1,16,3712]{2,1,0:T(8,128)(2,1)S(1)}, bf16[1,16,3712]{2,1,0:T(8,128)(2,1)S(1)}, u32[]{:S(2)}, u32[]{:S(2)}) collective-permute-start(bf16[1,16,3712]{2,1,0:T(8,128)(2,1)S(1)} %pack.1.refs_4_.refs_0_), channel_id=1, source_target_pairs={{0,1},{1,0},{2,3},{3,2},{4,5},{5,4},{6,7},{7,6},{8,9},{9,8},{10,11... | collective-permute-start | bytes 356360 | tf_op jit(solution)/shard_map/ppermute | solution.py:23
  9.1 7.9 %collective-permute-start.6 = (bf16[1,16,3712]{2,1,0:T(8,128)(2,1)S(1)}, bf16[1,16,3712]{2,1,0:T(8,128)(2,1)S(1)}, u32[]{:S(2)}, u32[]{:S(2)}) collective-permute-start(bf16[1,16,3712]{2,1,0:T(8,128)(2,1)S(1)} %collective-permute-done.5.refs_6_), channel_id=1, source_target_pairs={{0,1},{1,0},{2,3},{3,2},{4,5},{5,4},{6,7},{7,6},{8,9},{9,8},{10,11... | collective-permute-start | bytes 356360 | tf_op jit(solution)/shard_map/ppermute | solution.py:23
  11.3 5.8 %collective-permute-start.4 = (bf16[1,16,3712]{2,1,0:T(8,128)(2,1)S(1)}, bf16[1,16,3712]{2,1,0:T(8,128)(2,1)S(1)}, u32[]{:S(2)}, u32[]{:S(2)}) collective-permute-start(bf16[1,16,3712]{2,1,0:T(8,128)(2,1)S(1)} %collective-permute-done.3.refs_4_), channel_id=1, source_target_pairs={{0,1},{1,0},{2,3},{3,2},{4,5},{5,4},{6,7},{7,6},{8,9},{9,8},{10,11... | collective-permute-start | bytes 356360 | tf_op jit(solution)/shard_map/ppermute | solution.py:23
  11.5 5.5 %collective-permute-start.2 = (bf16[1,16,3712]{2,1,0:T(8,128)(2,1)S(1)}, bf16[1,16,3712]{2,1,0:T(8,128)(2,1)S(1)}, u32[]{:S(2)}, u32[]{:S(2)}) collective-permute-start(bf16[1,16,3712]{2,1,0:T(8,128)(2,1)S(1)} %collective-permute-done.1.refs_2_), channel_id=1, source_target_pairs={{0,1},{1,0},{2,3},{3,2},{4,5},{5,4},{6,7},{7,6},{8,9},{9,8},{10,11... | collective-permute-start | bytes 356360 | tf_op jit(solution)/shard_map/ppermute | solution.py:23
  17.1 22.1 %copy-start = (bf16[1,8,3584]{2,1,0:T(8,128)(2,1)S(1)}, bf16[1,8,3584]{2,1,0:T(8,128)(2,1)}, u32[]{:S(2)}) copy-start(bf16[1,8,3584]{2,1,0:T(8,128)(2,1)} %param.8) | copy-start | bytes 172036
  17.1 22.1 %copy-start.1 = (bf16[1,8,3584]{2,1,0:T(8,128)(2,1)S(1)}, bf16[1,8,3584]{2,1,0:T(8,128)(2,1)}, u32[]{:S(2)}) copy-start(bf16[1,8,3584]{2,1,0:T(8,128)(2,1)} %param.9) | copy-start | bytes 172036
  28.7 1.4 %collective-permute-start.8 = (bf16[1,16,3584]{2,1,0:T(8,128)(2,1)S(1)}, bf16[1,16,3584]{2,1,0:T(8,128)(2,1)S(1)}, u32[]{:S(2)}, u32[]{:S(2)}) collective-permute-start(bf16[1,16,3584]{2,1,0:T(8,128)(2,1)S(1)} %get-tuple-element.21), channel_id=1, source_target_pairs={{0,1},{1,0},{2,3},{3,2},{4,5},{5,4},{6,7},{7,6},{8,9},{9,8},{10,11... | collective-permute-start | bytes 344072 | tf_op jit(solution)/shard_map/ppermute | solution.py:23
  29.1 4.9 %collective-permute-start.7 = (bf16[1,16,3584]{2,1,0:T(8,128)(2,1)S(1)}, bf16[1,16,3584]{2,1,0:T(8,128)(2,1)S(1)}, u32[]{:S(2)}, u32[]{:S(2)}) collective-permute-start(bf16[1,16,3584]{2,1,0:T(8,128)(2,1)S(1)} %get-tuple-element.19), channel_id=1, source_target_pairs={{0,1},{1,0},{2,3},{3,2},{4,5},{5,4},{6,7},{7,6},{8,9},{9,8},{10,11... | collective-permute-start | bytes 344072 | tf_op jit(solution)/shard_map/ppermute | solution.py:23
  29.3 2.7 %collective-permute-start.10 = (bf16[1,16,3584]{2,1,0:T(8,128)(2,1)S(1)}, bf16[1,16,3584]{2,1,0:T(8,128)(2,1)S(1)}, u32[]{:S(2)}, u32[]{:S(2)}) collective-permute-start(bf16[1,16,3584]{2,1,0:T(8,128)(2,1)S(1)} %get-tuple-element.23), channel_id=1, source_target_pairs={{0,1},{1,0},{2,3},{3,2},{4,5},{5,4},{6,7},{7,6},{8,9},{9,8},{10,11... | collective-permute-start | bytes 344072 | tf_op jit(solution)/shard_map/ppermute | solution.py:23
  29.6 3.9 %collective-permute-start.12 = (bf16[1,16,3584]{2,1,0:T(8,128)(2,1)S(1)}, bf16[1,16,3584]{2,1,0:T(8,128)(2,1)S(1)}, u32[]{:S(2)}, u32[]{:S(2)}) collective-permute-start(bf16[1,16,3584]{2,1,0:T(8,128)(2,1)S(1)} %get-tuple-element.25), channel_id=1, source_target_pairs={{0,1},{1,0},{2,3},{3,2},{4,5},{5,4},{6,7},{7,6},{8,9},{9,8},{10,11... | collective-permute-start | bytes 344072 | tf_op jit(solution)/shard_map/ppermute | solution.py:23
  30.2 7.0 %collective-permute-start.9 = (bf16[1,16,3584]{2,1,0:T(8,128)(2,1)S(1)}, bf16[1,16,3584]{2,1,0:T(8,128)(2,1)S(1)}, u32[]{:S(2)}, u32[]{:S(2)}) collective-permute-start(bf16[1,16,3584]{2,1,0:T(8,128)(2,1)S(1)} %add_convert_fusion.2), channel_id=1, source_target_pairs={{0,6},{1,7},{2,4},{3,5},{4,2},{5,3},{6,0},{7,1},{8,14},{9,15},{10,... | collective-permute-start | bytes 344072 | tf_op jit(solution)/shard_map/ppermute | solution.py:23
  32.1 6.9 %collective-permute-start.11 = (bf16[1,16,3584]{2,1,0:T(8,128)(2,1)S(1)}, bf16[1,16,3584]{2,1,0:T(8,128)(2,1)S(1)}, u32[]{:S(2)}, u32[]{:S(2)}) collective-permute-start(bf16[1,16,3584]{2,1,0:T(8,128)(2,1)S(1)} %add_convert_fusion.1), channel_id=1, source_target_pairs={{0,2},{1,3},{2,0},{3,1},{4,6},{5,7},{6,4},{7,5},{8,10},{9,11},{10,... | collective-permute-start | bytes 344072 | tf_op jit(solution)/shard_map/ppermute | solution.py:23
  33.6 5.5 %collective-permute-start.13 = (bf16[1,16,3584]{2,1,0:T(8,128)(2,1)S(1)}, bf16[1,16,3584]{2,1,0:T(8,128)(2,1)S(1)}, u32[]{:S(2)}, u32[]{:S(2)}) collective-permute-start(bf16[1,16,3584]{2,1,0:T(8,128)(2,1)S(1)} %add_convert_fusion), channel_id=1, source_target_pairs={{0,4},{1,5},{2,6},{3,7},{4,0},{5,1},{6,2},{7,3},{8,12},{9,13},{10,... | collective-permute-start | bytes 344072 | tf_op jit(solution)/shard_map/ppermute | solution.py:23
  39.2 5.1 %collective-permute-start.15 = (bf16[8,3584]{1,0:T(8,128)(2,1)S(1)}, bf16[8,3584]{1,0:T(8,128)(2,1)S(1)}, u32[]{:S(2)}, u32[]{:S(2)}) collective-permute-start(bf16[8,3584]{1,0:T(8,128)(2,1)S(1)} %get-tuple-element.26), channel_id=1, source_target_pairs={{8,16},{16,8},{9,17},{17,9},{10,18},{18,10},{11,19},{19,11},{12,20... | collective-permute-start | bytes 172040 | tf_op jit(solution)/shard_map/ppermute | solution.py:287
  39.9 6.6 %collective-permute-start.14 = (bf16[8,3584]{1,0:T(8,128)(2,1)S(1)}, bf16[8,3584]{1,0:T(8,128)(2,1)S(1)}, u32[]{:S(2)}, u32[]{:S(2)}) collective-permute-start(bf16[8,3584]{1,0:T(8,128)(2,1)S(1)} %get-tuple-element.27), channel_id=1, source_target_pairs={{0,8},{8,0},{16,24},{24,16},{1,9},{9,1},{17,25},{25,17},{2,10},{10... | collective-permute-start | bytes 172040 | tf_op jit(solution)/shard_map/ppermute | solution.py:287
where the time goes:
time: 47.3 us; the launch traced here: 47.1 us
  Pallas kernels  17.7 us (37%)
  starting transfers between devices  14.8 us (31%)
  waiting for transfers between devices  13 us (27%)
  other arithmetic  0.86 us (2%)
  between operations  0.76 us (2%)
    pallas_call x1, Pallas kernels, experts(): pl.pallas_call(functools.partial(expert_kernel, top), out_shape=[jax.Shap...  11.6 us
    ppermute x14, waiting for transfers between devices, flip(): return lax.ppermute(value, 'expert', [(i, i ^ bit) for i in range(count)])  10.8 us
    ppermute x14, starting transfers between devices, flip(): return lax.ppermute(value, 'expert', [(i, i ^ bit) for i in range(count)])  9.67 us
    pallas_call x1, Pallas kernels, fetch(): pl.pallas_call(fetch_kernel, out_shape=[pltpu.VMEM(a.shape, a.dtype) for...  5.21 us
    ppermute x2, starting transfers between devices, trade(): return lax.ppermute(value, 'pipe', pairs)  5.13 us
    ppermute x2, waiting for transfers between devices, trade(): return lax.ppermute(value, 'pipe', pairs)  2.16 us
  transfers between devices with their start and end apart: 16, of which 7 were waited for; matrix products, arithmetic and copies ran while one was open for 0% of the time, Pallas kernels for 11%

commit v1 on v0

--- a/solution.py
+++ b/solution.py
@@ -98,8 +98,9 @@
 
 
 def expert_kernel(top, me_ref, gain_ref, router_ref, wg_ref, wu_ref, wd_hbm, *refs):
-    pieces, outs = refs[:8], refs[8:16]
-    nb, sg, gate_s, up_s, out_s, hid_s, dg_s, du_s, route_s, wd_ref, wd_sem = refs[16:]
+    pieces, evens, last, rest = refs[:8], refs[8:12], refs[12], refs[13]
+    outs = [evens[q // 2] if q % 2 == 0 else last if q == 7 else rest.at[q // 2] for q in range(8)]
+    nb, sg, gate_s, up_s, out_s, hid_s, dg_s, du_s, route_s, wd_ref, wd_sem = refs[14:]
     wd_copy = pltpu.make_async_copy(wd_hbm, wd_ref, wd_sem)
     wd_copy.start()
     blocks, double, _ = pieces[0].shape
@@ -213,9 +214,10 @@
     total = 8 * double // 2
     return pl.pallas_call(
         functools.partial(expert_kernel, top),
-        out_shape=[jax.ShapeDtypeStruct((blocks, double, width), BF16)] * 8,
+        out_shape=[jax.ShapeDtypeStruct((blocks, double, width), BF16)] * 5
+        + [jax.ShapeDtypeStruct((3, blocks, double, width), BF16)],
         in_specs=[SMEM] + [VMEM] * 4 + [HBM] + [VMEM] * 8,
-        out_specs=[VMEM] * 8,
+        out_specs=[VMEM] * 6,
         scratch_shapes=[
             pltpu.VMEM((total, width), BF16),
             pltpu.VMEM((total, width), BF16),
@@ -262,7 +264,11 @@
         ids.shape[1], me, gain, route, wg, wu, pltpu.with_memory_space_constraint(w_down[0], pltpu.HBM),
         [pieces[j] for j in range(8)],
     )
-    kept = {j: add(outs[j], flip(outs[j + 1], 1)) for j in (6, 2, 4, 0)}
+    evens, last, rest = outs[:4], outs[4], outs[5]
+    kept = {6: add(evens[3], flip(last, 1))}
+    rest = flip(rest, 1)
+    for j in (2, 4, 0):
+        kept[j] = add(evens[j // 2], rest[j // 2])
     came = [flip(kept[j], j) for j in (6, 2, 4)]
     if count > 8:
         got = kept[0].astype(F32) + sum(c.astype(F32) for c in came)

time: 47.3 us -> 47.1 us (level)
  starting transfers between devices: 14.8 us -> 14.2 us
  waiting for transfers between devices: 13 us -> 13.5 us
    ppermute x14 -> x12, waiting for transfers between devices: 10.8 us -> 11.4 us  [flip(): return lax.ppermute(value, 'expert', [(i, i ^ bit) for i in range(count)])]
    ppermute x14 -> x12, starting transfers between devices: 9.67 us -> 9.1 us  [flip(): return lax.ppermute(value, 'expert', [(i, i ^ bit) for i in range(count)])]
  transfers between devices with their start and end apart: 16 -> 14, of which waited for: 7 -> 7; matrix products, arithmetic and copies ran while one was open for 0% -> 0% of each run, Pallas kernels for 11% -> 11%
where the time goes in v1:
time: 47.1 us; the launch traced here: 46.9 us
  Pallas kernels  17.5 us (37%)
  starting transfers between devices  14.2 us (30%)
  waiting for transfers between devices  13.5 us (29%)
  other arithmetic  0.85 us (2%)
  between operations  0.75 us (2%)
    ppermute x12, waiting for transfers between devices, flip(): return lax.ppermute(value, 'expert', [(i, i ^ bit) for i in range(count)])  11.4 us
    pallas_call x1, Pallas kernels, experts(): pl.pallas_call(functools.partial(expert_kernel, top), out_shape=[jax.Shap...  11.4 us
    ppermute x12, starting transfers between devices, flip(): return lax.ppermute(value, 'expert', [(i, i ^ bit) for i in range(count)])  9.1 us
    pallas_call x1, Pallas kernels, fetch(): pl.pallas_call(fetch_kernel, out_shape=[pltpu.VMEM(a.shape, a.dtype) for...  5.21 us
    ppermute x2, starting transfers between devices, trade(): return lax.ppermute(value, 'pipe', pairs)  5.12 us
    ppermute x2, waiting for transfers between devices, trade(): return lax.ppermute(value, 'pipe', pairs)  2.16 us
  transfers between devices with their start and end apart: 14, of which 7 were waited for; matrix products, arithmetic and copies ran while one was open for 0% of the time, Pallas kernels for 11%

profile of v1, /device:TPU:0, one launch (start us, length us, event | category | flops | bytes accessed | tf_op | source)
XLA Modules:
  0.0 46.9 jit_solution(10275180256909294513)
XLA Ops:
  0.6 0.9 %pack.1.refs_4_.refs_0_ = bf16[1,16,3712]{2,1,0:T(8,128)(2,1)S(1)} custom-call(bf16[8,3584]{1,0:T(8,128)(2,1)} %bitcast.64, bf16[8,3584]{1,0:T(8,128)(2,1)} %bitcast.65, s32[2,8]{1,0:T(2,128)} %bitcast.67), custom_call_target="tpu_custom_call" | custom-call | bytes 229376 | tf_op jit(solution)/shard_map/pack/pallas_call | solution.py:52
  1.5 4.0 %collective-permute-start.5 = (bf16[1,16,3712]{2,1,0:T(8,128)(2,1)S(1)}, bf16[1,16,3712]{2,1,0:T(8,128)(2,1)S(1)}, u32[]{:S(2)}, u32[]{:S(2)}) collective-permute-start(bf16[1,16,3712]{2,1,0:T(8,128)(2,1)S(1)} %pack.1.refs_4_.refs_0_), channel_id=1, source_target_pairs={{0,6},{1,7},{2,4},{3,5},{4,2},{5,3},{6,0},{7,1},{8,14},{9,15},{10,... | collective-permute-start | bytes 356360 | tf_op jit(solution)/shard_map/ppermute | solution.py:23
  5.5 0.5 %collective-permute-start.3 = (bf16[1,16,3712]{2,1,0:T(8,128)(2,1)S(1)}, bf16[1,16,3712]{2,1,0:T(8,128)(2,1)S(1)}, u32[]{:S(2)}, u32[]{:S(2)}) collective-permute-start(bf16[1,16,3712]{2,1,0:T(8,128)(2,1)S(1)} %pack.1.refs_4_.refs_0_), channel_id=1, source_target_pairs={{0,4},{1,5},{2,6},{3,7},{4,0},{5,1},{6,2},{7,3},{8,12},{9,13},{10,... | collective-permute-start | bytes 356360 | tf_op jit(solution)/shard_map/ppermute | solution.py:23
  6.0 0.1 collective-permute-start.1
  6.2 0.0 collective-permute-start
  6.2 3.0 %collective-permute-done.5.refs_6_ = bf16[1,16,3712]{2,1,0:T(8,128)(2,1)S(1)} collective-permute-done((bf16[1,16,3712]{2,1,0:T(8,128)(2,1)S(1)}, bf16[1,16,3712]{2,1,0:T(8,128)(2,1)S(1)}, u32[]{:S(2)}, u32[]{:S(2)}) %collective-permute-start.5) | collective-permute-done | bytes 118816 | tf_op jit(solution)/shard_map/ppermute | solution.py:23
  9.1 0.0 collective-permute-start.6
  9.1 2.2 %collective-permute-done.3.refs_4_ = bf16[1,16,3712]{2,1,0:T(8,128)(2,1)S(1)} collective-permute-done((bf16[1,16,3712]{2,1,0:T(8,128)(2,1)S(1)}, bf16[1,16,3712]{2,1,0:T(8,128)(2,1)S(1)}, u32[]{:S(2)}, u32[]{:S(2)}) %collective-permute-start.3) | collective-permute-done | bytes 118816 | tf_op jit(solution)/shard_map/ppermute | solution.py:23
  11.3 0.0 collective-permute-start.4
  11.3 0.2 collective-permute-done.1.refs_2_
  11.5 0.3 collective-permute-start.2
  11.8 5.2 %fetch.1 = (bf16[3584,1024]{1,0:T(8,128)(2,1)S(1)}, bf16[3584,1024]{1,0:T(8,128)(2,1)S(1)}, f32[8,3584]{1,0:T(8,128)S(1)}, f32[1,3584]{1,0:T(1,128)S(1)}) custom-call(bf16[3584,1024]{1,0:T(8,128)(2,1)} %bitcast.61, bf16[3584,1024]{1,0:T(8,128)(2,1)} %bitcast.62, f32[8,3584]{1,0:T(8,128)} %bitcast.66, f32[1,3584]{1,0:T(1,128)} %refs_3_.1, ...), custom_call_target="tpu_custom_call" | custom-call | bytes 14809088 | tf_op jit(solution)/shard_map/fetch/pallas_call | solution.py:77
  17.0 0.0 collective-permute-done.refs_1_
  17.0 0.0 collective-permute-done.6.refs_7_
  17.0 0.0 collective-permute-done.4.refs_5_
  17.1 0.0 collective-permute-done.2.refs_3_
  17.1 0.0 copy-start
  17.1 0.0 copy-start.1
  17.1 11.4 %experts.1 = (bf16[1,16,3584]{2,1,0:T(8,128)(2,1)S(1)}, bf16[1,16,3584]{2,1,0:T(8,128)(2,1)S(1)}, bf16[1,16,3584]{2,1,0:T(8,128)(2,1)S(1)}, bf16[1,16,3584]{2,1,...) custom-call(s32[1]{0:T(128)} %bitcast.1.refs_5_.me_ref, ...), custom_call_target="tpu_custom_call" | custom-call | tf_op jit(solution)/shard_map/experts/pallas_call | solution.py:215
  28.5 0.3 collective-permute-start.8
  28.8 0.3 collective-permute-start.7
  29.1 0.8 %collective-permute-done.8 = bf16[1,16,3584]{2,1,0:T(8,128)(2,1)S(1)} collective-permute-done((bf16[1,16,3584]{2,1,0:T(8,128)(2,1)S(1)}, bf16[1,16,3584]{2,1,0:T(8,128)(2,1)S(1)}, u32[]{:S(2)}, u32[]{:S(2)}) %collective-permute-start.8) | collective-permute-done | bytes 114720 | tf_op jit(solution)/shard_map/ppermute | solution.py:23
  29.9 1.9 %collective-permute-start.9 = (bf16[1,16,3584]{2,1,0:T(8,128)(2,1)S(1)}, bf16[1,16,3584]{2,1,0:T(8,128)(2,1)S(1)}, u32[]{:S(2)}, u32[]{:S(2)}) collective-permute-start(bf16[1,16,3584]{2,1,0:T(8,128)(2,1)S(1)} %add_convert_fusion), channel_id=1, source_target_pairs={{0,6},{1,7},{2,4},{3,5},{4,2},{5,3},{6,0},{7,1},{8,14},{9,15},{10,... | collective-permute-start | bytes 344072 | tf_op jit(solution)/shard_map/ppermute | solution.py:23
  31.8 0.0 collective-permute-done.7
  31.8 0.1 fusion.1
  31.9 1.4 %collective-permute-start.10 = (bf16[1,16,3584]{2,1,0:T(8,128)(2,1)S(1)}, bf16[1,16,3584]{2,1,0:T(8,128)(2,1)S(1)}, u32[]{:S(2)}, u32[]{:S(2)}) collective-permute-start(bf16[1,16,3584]{2,1,0:T(8,128)(2,1)S(1)} %get-tuple-element.24), channel_id=1, source_target_pairs={{0,2},{1,3},{2,0},{3,1},{4,6},{5,7},{6,4},{7,5},{8,10},{9,11},{10,... | collective-permute-start | bytes 344072 | tf_op jit(solution)/shard_map/ppermute | solution.py:23
  33.3 0.3 collective-permute-start.11
  33.6 3.3 %collective-permute-done.9 = bf16[1,16,3584]{2,1,0:T(8,128)(2,1)S(1)} collective-permute-done((bf16[1,16,3584]{2,1,0:T(8,128)(2,1)S(1)}, bf16[1,16,3584]{2,1,0:T(8,128)(2,1)S(1)}, u32[]{:S(2)}, u32[]{:S(2)}) %collective-permute-start.9) | collective-permute-done | bytes 114720 | tf_op jit(solution)/shard_map/ppermute | solution.py:23
  36.9 1.9 %collective-permute-done.10 = bf16[1,16,3584]{2,1,0:T(8,128)(2,1)S(1)} collective-permute-done((bf16[1,16,3584]{2,1,0:T(8,128)(2,1)S(1)}, bf16[1,16,3584]{2,1,0:T(8,128)(2,1)S(1)}, u32[]{:S(2)}, u32[]{:S(2)}) %collective-permute-start.10) | collective-permute-done | bytes 114720 | tf_op jit(solution)/shard_map/ppermute | solution.py:23
  38.8 0.0 collective-permute-done.11
  38.8 0.1 add_add_fusion
  38.9 0.0 copy-done
  38.9 0.0 copy-done.1
  38.9 0.7 %collective-permute-start.13 = (bf16[8,3584]{1,0:T(8,128)(2,1)S(1)}, bf16[8,3584]{1,0:T(8,128)(2,1)S(1)}, u32[]{:S(2)}, u32[]{:S(2)}) collective-permute-start(bf16[8,3584]{1,0:T(8,128)(2,1)S(1)} %get-tuple-element.22), channel_id=1, source_target_pairs={{8,16},{16,8},{9,17},{17,9},{10,18},{18,10},{11,19},{19,11},{12,20... | collective-permute-start | bytes 172040 | tf_op jit(solution)/shard_map/ppermute | solution.py:293
  39.6 4.5 %collective-permute-start.12 = (bf16[8,3584]{1,0:T(8,128)(2,1)S(1)}, bf16[8,3584]{1,0:T(8,128)(2,1)S(1)}, u32[]{:S(2)}, u32[]{:S(2)}) collective-permute-start(bf16[8,3584]{1,0:T(8,128)(2,1)S(1)} %get-tuple-element.23), channel_id=1, source_target_pairs={{0,8},{8,0},{16,24},{24,16},{1,9},{9,1},{17,25},{25,17},{2,10},{10... | collective-permute-start | bytes 172040 | tf_op jit(solution)/shard_map/ppermute | solution.py:293
  44.0 0.0 collective-permute-done.13
  44.0 2.2 %collective-permute-done.12 = bf16[8,3584]{1,0:T(8,128)(2,1)S(1)} collective-permute-done((bf16[8,3584]{1,0:T(8,128)(2,1)S(1)}, bf16[8,3584]{1,0:T(8,128)(2,1)S(1)}, u32[]{:S(2)}, u32[]{:S(2)}) %collective-permute-start.12) | collective-permute-done | bytes 57376 | tf_op jit(solution)/shard_map/ppermute | solution.py:293
  46.2 0.7 %select_bitcast_fusion = (bf16[1,8,3584]{2,1,0:T(8,128)(2,1)}, bf16[1,8,3584]{2,1,0:T(8,128)(2,1)}) fusion(bf16[8,3584]{1,0:T(8,128)(2,1)S(1)} %collective-permute-done.13, bf16[8,3584]{1,0:T(8,128)(2,1)S(1)} %collective-permute-done.12, pred[]{:T(512)S(6)} %eq.5), kind=kLoop, calls=%fused_computation.17 | loop fusion | flops 57344 | bytes 229377 | tf_op jit(solution)/shard_map/broadcast_in_dim | solution.py:299
  (2 shorter events, 0.1 us)
Async XLA Ops:
  1.5 7.6 %collective-permute-start.5 = (bf16[1,16,3712]{2,1,0:T(8,128)(2,1)S(1)}, bf16[1,16,3712]{2,1,0:T(8,128)(2,1)S(1)}, u32[]{:S(2)}, u32[]{:S(2)}) collective-permute-start(bf16[1,16,3712]{2,1,0:T(8,128)(2,1)S(1)} %pack.1.refs_4_.refs_0_), channel_id=1, source_target_pairs={{0,6},{1,7},{2,4},{3,5},{4,2},{5,3},{6,0},{7,1},{8,14},{9,15},{10,... | collective-permute-start | bytes 356360 | tf_op jit(solution)/shard_map/ppermute | solution.py:23
  5.5 5.8 %collective-permute-start.3 = (bf16[1,16,3712]{2,1,0:T(8,128)(2,1)S(1)}, bf16[1,16,3712]{2,1,0:T(8,128)(2,1)S(1)}, u32[]{:S(2)}, u32[]{:S(2)}) collective-permute-start(bf16[1,16,3712]{2,1,0:T(8,128)(2,1)S(1)} %pack.1.refs_4_.refs_0_), channel_id=1, source_target_pairs={{0,4},{1,5},{2,6},{3,7},{4,0},{5,1},{6,2},{7,3},{8,12},{9,13},{10,... | collective-permute-start | bytes 356360 | tf_op jit(solution)/shard_map/ppermute | solution.py:23
  6.0 5.5 %collective-permute-start.1 = (bf16[1,16,3712]{2,1,0:T(8,128)(2,1)S(1)}, bf16[1,16,3712]{2,1,0:T(8,128)(2,1)S(1)}, u32[]{:S(2)}, u32[]{:S(2)}) collective-permute-start(bf16[1,16,3712]{2,1,0:T(8,128)(2,1)S(1)} %pack.1.refs_4_.refs_0_), channel_id=1, source_target_pairs={{0,2},{1,3},{2,0},{3,1},{4,6},{5,7},{6,4},{7,5},{8,10},{9,11},{10,... | collective-permute-start | bytes 356360 | tf_op jit(solution)/shard_map/ppermute | solution.py:23
  6.2 10.9 %collective-permute-start = (bf16[1,16,3712]{2,1,0:T(8,128)(2,1)S(1)}, bf16[1,16,3712]{2,1,0:T(8,128)(2,1)S(1)}, u32[]{:S(2)}, u32[]{:S(2)}) collective-permute-start(bf16[1,16,3712]{2,1,0:T(8,128)(2,1)S(1)} %pack.1.refs_4_.refs_0_), channel_id=1, source_target_pairs={{0,1},{1,0},{2,3},{3,2},{4,5},{5,4},{6,7},{7,6},{8,9},{9,8},{10,11... | collective-permute-start | bytes 356360 | tf_op jit(solution)/shard_map/ppermute | solution.py:23
  9.1 7.9 %collective-permute-start.6 = (bf16[1,16,3712]{2,1,0:T(8,128)(2,1)S(1)}, bf16[1,16,3712]{2,1,0:T(8,128)(2,1)S(1)}, u32[]{:S(2)}, u32[]{:S(2)}) collective-permute-start(bf16[1,16,3712]{2,1,0:T(8,128)(2,1)S(1)} %collective-permute-done.5.refs_6_), channel_id=1, source_target_pairs={{0,1},{1,0},{2,3},{3,2},{4,5},{5,4},{6,7},{7,6},{8,9},{9,8},{10,11... | collective-permute-start | bytes 356360 | tf_op jit(solution)/shard_map/ppermute | solution.py:23
  11.3 5.8 %collective-permute-start.4 = (bf16[1,16,3712]{2,1,0:T(8,128)(2,1)S(1)}, bf16[1,16,3712]{2,1,0:T(8,128)(2,1)S(1)}, u32[]{:S(2)}, u32[]{:S(2)}) collective-permute-start(bf16[1,16,3712]{2,1,0:T(8,128)(2,1)S(1)} %collective-permute-done.3.refs_4_), channel_id=1, source_target_pairs={{0,1},{1,0},{2,3},{3,2},{4,5},{5,4},{6,7},{7,6},{8,9},{9,8},{10,11... | collective-permute-start | bytes 356360 | tf_op jit(solution)/shard_map/ppermute | solution.py:23
  11.5 5.5 %collective-permute-start.2 = (bf16[1,16,3712]{2,1,0:T(8,128)(2,1)S(1)}, bf16[1,16,3712]{2,1,0:T(8,128)(2,1)S(1)}, u32[]{:S(2)}, u32[]{:S(2)}) collective-permute-start(bf16[1,16,3712]{2,1,0:T(8,128)(2,1)S(1)} %collective-permute-done.1.refs_2_), channel_id=1, source_target_pairs={{0,1},{1,0},{2,3},{3,2},{4,5},{5,4},{6,7},{7,6},{8,9},{9,8},{10,11... | collective-permute-start | bytes 356360 | tf_op jit(solution)/shard_map/ppermute | solution.py:23
  17.1 21.8 %copy-start = (bf16[1,8,3584]{2,1,0:T(8,128)(2,1)S(1)}, bf16[1,8,3584]{2,1,0:T(8,128)(2,1)}, u32[]{:S(2)}) copy-start(bf16[1,8,3584]{2,1,0:T(8,128)(2,1)} %param.8) | copy-start | bytes 172036
  17.1 21.8 %copy-start.1 = (bf16[1,8,3584]{2,1,0:T(8,128)(2,1)S(1)}, bf16[1,8,3584]{2,1,0:T(8,128)(2,1)}, u32[]{:S(2)}) copy-start(bf16[1,8,3584]{2,1,0:T(8,128)(2,1)} %param.9) | copy-start | bytes 172036
  28.5 1.4 %collective-permute-start.8 = (bf16[1,16,3584]{2,1,0:T(8,128)(2,1)S(1)}, bf16[1,16,3584]{2,1,0:T(8,128)(2,1)S(1)}, u32[]{:S(2)}, u32[]{:S(2)}) collective-permute-start(bf16[1,16,3584]{2,1,0:T(8,128)(2,1)S(1)} %get-tuple-element.19), channel_id=1, source_target_pairs={{0,1},{1,0},{2,3},{3,2},{4,5},{5,4},{6,7},{7,6},{8,9},{9,8},{10,11... | collective-permute-start | bytes 344072 | tf_op jit(solution)/shard_map/ppermute | solution.py:23
  28.8 3.0 %collective-permute-start.7 = (bf16[3,1,16,3584]{3,2,1,0:T(8,128)(2,1)S(1)}, bf16[3,1,16,3584]{3,2,1,0:T(8,128)(2,1)S(1)}, u32[]{:S(2)}, u32[]{:S(2)}) collective-permute-start(bf16[3,1,16,3584]{3,2,1,0:T(8,128)(2,1)S(1)} %get-tuple-element.17), channel_id=1, source_target_pairs={{0,1},{1,0},{2,3},{3,2},{4,5},{5,4},{6,7},{7,6},{8,9},{9,8},{10,11... | collective-permute-start | bytes 1032200 | tf_op jit(solution)/shard_map/ppermute | solution.py:23
  29.9 7.0 %collective-permute-start.9 = (bf16[1,16,3584]{2,1,0:T(8,128)(2,1)S(1)}, bf16[1,16,3584]{2,1,0:T(8,128)(2,1)S(1)}, u32[]{:S(2)}, u32[]{:S(2)}) collective-permute-start(bf16[1,16,3584]{2,1,0:T(8,128)(2,1)S(1)} %add_convert_fusion), channel_id=1, source_target_pairs={{0,6},{1,7},{2,4},{3,5},{4,2},{5,3},{6,0},{7,1},{8,14},{9,15},{10,... | collective-permute-start | bytes 344072 | tf_op jit(solution)/shard_map/ppermute | solution.py:23
  31.9 6.9 %collective-permute-start.10 = (bf16[1,16,3584]{2,1,0:T(8,128)(2,1)S(1)}, bf16[1,16,3584]{2,1,0:T(8,128)(2,1)S(1)}, u32[]{:S(2)}, u32[]{:S(2)}) collective-permute-start(bf16[1,16,3584]{2,1,0:T(8,128)(2,1)S(1)} %get-tuple-element.24), channel_id=1, source_target_pairs={{0,2},{1,3},{2,0},{3,1},{4,6},{5,7},{6,4},{7,5},{8,10},{9,11},{10,... | collective-permute-start | bytes 344072 | tf_op jit(solution)/shard_map/ppermute | solution.py:23
  33.3 5.5 %collective-permute-start.11 = (bf16[1,16,3584]{2,1,0:T(8,128)(2,1)S(1)}, bf16[1,16,3584]{2,1,0:T(8,128)(2,1)S(1)}, u32[]{:S(2)}, u32[]{:S(2)}) collective-permute-start(bf16[1,16,3584]{2,1,0:T(8,128)(2,1)S(1)} %get-tuple-element.25), channel_id=1, source_target_pairs={{0,4},{1,5},{2,6},{3,7},{4,0},{5,1},{6,2},{7,3},{8,12},{9,13},{10,... | collective-permute-start | bytes 344072 | tf_op jit(solution)/shard_map/ppermute | solution.py:23
  38.9 5.1 %collective-permute-start.13 = (bf16[8,3584]{1,0:T(8,128)(2,1)S(1)}, bf16[8,3584]{1,0:T(8,128)(2,1)S(1)}, u32[]{:S(2)}, u32[]{:S(2)}) collective-permute-start(bf16[8,3584]{1,0:T(8,128)(2,1)S(1)} %get-tuple-element.22), channel_id=1, source_target_pairs={{8,16},{16,8},{9,17},{17,9},{10,18},{18,10},{11,19},{19,11},{12,20... | collective-permute-start | bytes 172040 | tf_op jit(solution)/shard_map/ppermute | solution.py:293
  39.6 6.6 %collective-permute-start.12 = (bf16[8,3584]{1,0:T(8,128)(2,1)S(1)}, bf16[8,3584]{1,0:T(8,128)(2,1)S(1)}, u32[]{:S(2)}, u32[]{:S(2)}) collective-permute-start(bf16[8,3584]{1,0:T(8,128)(2,1)S(1)} %get-tuple-element.23), channel_id=1, source_target_pairs={{0,8},{8,0},{16,24},{24,16},{1,9},{9,1},{17,25},{25,17},{2,10},{10... | collective-permute-start | bytes 172040 | tf_op jit(solution)/shard_map/ppermute | solution.py:293

commit v2 on v1

--- a/solution.py
+++ b/solution.py
@@ -248,7 +248,9 @@
     rows, _ = x.shape
     count = lax.axis_size("expert")
     groups = count // EXPERTS
-    me = (lax.axis_index("expert") // groups).astype(jnp.int32).reshape(1)
+    index = lax.axis_index("expert")
+    stage = lax.axis_index("pipe")
+    me = jnp.stack([index // groups, index, stage]).astype(jnp.int32)
     own = pack(x, dy, ids.T)
     bit = 8
     while bit < count:
@@ -264,6 +266,7 @@
         ids.shape[1], me, gain, route, wg, wu, pltpu.with_memory_space_constraint(w_down[0], pltpu.HBM),
         [pieces[j] for j in range(8)],
     )
+    outs, index, stage = lax.optimization_barrier((outs, index, stage))
     evens, last, rest = outs[:4], outs[4], outs[5]
     kept = {6: add(evens[3], flip(last, 1))}
     rest = flip(rest, 1)
@@ -282,15 +285,17 @@
     section_out = (x.astype(F32) + got[0, :rows]).astype(BF16)
     section_grad = (dy.astype(F32) + got[0, rows:]).astype(BF16)
     stages = lax.axis_size("pipe")
-    odd = lax.axis_index("pipe") % 2 == 1
+    odd = lax.rem(stage + index, 2) == 1
     first = jnp.where(odd, section_grad, section_out)
     second = jnp.where(odd, section_out, section_grad)
 
     def trade(value, parity):
         pairs = []
-        for s in range(parity, stages - 1, 2):
-            pairs += [(s, s + 1), (s + 1, s)]
-        return lax.ppermute(value, "pipe", pairs)
+        for s in range(stages - 1):
+            for i in range((s + parity) % 2, count, 2):
+                low, high = s * count + i, (s + 1) * count + i
+                pairs += [(low, high), (high, low)]
+        return lax.ppermute(value, ("pipe", "expert"), pairs)
 
     first = trade(first, 0)
     second = trade(second, 1)

time: 47.1 us -> 49.7 us (1.055)
  starting transfers between devices: 14.2 us -> 16.1 us
  Pallas kernels: 17.5 us -> 18.2 us
    ppermute x2, starting transfers between devices: 5.12 us -> 6.97 us  [trade(): return lax.ppermute(value, ('pipe', 'expert'), pairs)]
    pallas_call x1, Pallas kernels: 5.21 us -> 5.75 us  [fetch(): pl.pallas_call(fetch_kernel, out_shape=[pltpu.VMEM(a.shape, a.dtype) for...]
  transfers between devices with their start and end apart: 14 -> 14, of which waited for: 7 -> 7; matrix products, arithmetic and copies ran while one was open for 0% -> 0% of each run, Pallas kernels for 11% -> 12%
where the time goes in v2:
time: 49.7 us; the launch traced here: 49.5 us
  Pallas kernels  18.2 us (37%)
  starting transfers between devices  16.1 us (32%)
  waiting for transfers between devices  13.5 us (27%)
  other arithmetic  0.93 us (2%)
  between operations  0.77 us (2%)
    pallas_call x1, Pallas kernels, experts(): pl.pallas_call(functools.partial(expert_kernel, top), out_shape=[jax.Shap...  11.6 us
    ppermute x12, waiting for transfers between devices, flip(): return lax.ppermute(value, 'expert', [(i, i ^ bit) for i in range(count)])  11.4 us
    ppermute x12, starting transfers between devices, flip(): return lax.ppermute(value, 'expert', [(i, i ^ bit) for i in range(count)])  9.1 us
    ppermute x2, starting transfers between devices, trade(): return lax.ppermute(value, ('pipe', 'expert'), pairs)  6.97 us
    pallas_call x1, Pallas kernels, fetch(): pl.pallas_call(fetch_kernel, out_shape=[pltpu.VMEM(a.shape, a.dtype) for...  5.75 us
    ppermute x2, waiting for transfers between devices, trade(): return lax.ppermute(value, ('pipe', 'expert'), pairs)  2.13 us
  transfers between devices with their start and end apart: 14, of which 7 were waited for; matrix products, arithmetic and copies ran while one was open for 0% of the time, Pallas kernels for 12%

profile of v2, /device:TPU:0, one launch (start us, length us, event | category | flops | bytes accessed | tf_op | source)
XLA Modules:
  0.0 49.5 jit_solution(11296583122470267086)
XLA Ops:
  0.6 0.9 %pack.1.refs_4_.refs_0_ = bf16[1,16,3712]{2,1,0:T(8,128)(2,1)S(1)} custom-call(bf16[8,3584]{1,0:T(8,128)(2,1)} %bitcast.65, bf16[8,3584]{1,0:T(8,128)(2,1)} %bitcast.66, s32[2,8]{1,0:T(2,128)} %bitcast.68), custom_call_target="tpu_custom_call" | custom-call | bytes 229376 | tf_op jit(solution)/shard_map/pack/pallas_call | solution.py:52
  1.5 4.0 %collective-permute-start.5 = (bf16[1,16,3712]{2,1,0:T(8,128)(2,1)S(1)}, bf16[1,16,3712]{2,1,0:T(8,128)(2,1)S(1)}, u32[]{:S(2)}, u32[]{:S(2)}) collective-permute-start(bf16[1,16,3712]{2,1,0:T(8,128)(2,1)S(1)} %pack.1.refs_4_.refs_0_), channel_id=1, source_target_pairs={{0,6},{1,7},{2,4},{3,5},{4,2},{5,3},{6,0},{7,1},{8,14},{9,15},{10,... | collective-permute-start | bytes 356360 | tf_op jit(solution)/shard_map/ppermute | solution.py:23
  5.5 0.5 %collective-permute-start.3 = (bf16[1,16,3712]{2,1,0:T(8,128)(2,1)S(1)}, bf16[1,16,3712]{2,1,0:T(8,128)(2,1)S(1)}, u32[]{:S(2)}, u32[]{:S(2)}) collective-permute-start(bf16[1,16,3712]{2,1,0:T(8,128)(2,1)S(1)} %pack.1.refs_4_.refs_0_), channel_id=1, source_target_pairs={{0,4},{1,5},{2,6},{3,7},{4,0},{5,1},{6,2},{7,3},{8,12},{9,13},{10,... | collective-permute-start | bytes 356360 | tf_op jit(solution)/shard_map/ppermute | solution.py:23
  6.0 0.1 collective-permute-start.1
  6.2 0.0 collective-permute-start
  6.2 3.0 %collective-permute-done.5.refs_6_ = bf16[1,16,3712]{2,1,0:T(8,128)(2,1)S(1)} collective-permute-done((bf16[1,16,3712]{2,1,0:T(8,128)(2,1)S(1)}, bf16[1,16,3712]{2,1,0:T(8,128)(2,1)S(1)}, u32[]{:S(2)}, u32[]{:S(2)}) %collective-permute-start.5) | collective-permute-done | bytes 118816 | tf_op jit(solution)/shard_map/ppermute | solution.py:23
  9.1 0.0 collective-permute-start.6
  9.1 2.2 %collective-permute-done.3.refs_4_ = bf16[1,16,3712]{2,1,0:T(8,128)(2,1)S(1)} collective-permute-done((bf16[1,16,3712]{2,1,0:T(8,128)(2,1)S(1)}, bf16[1,16,3712]{2,1,0:T(8,128)(2,1)S(1)}, u32[]{:S(2)}, u32[]{:S(2)}) %collective-permute-start.3) | collective-permute-done | bytes 118816 | tf_op jit(solution)/shard_map/ppermute | solution.py:23
  11.3 0.0 collective-permute-start.4
  11.3 0.2 collective-permute-done.1.refs_2_
  11.5 0.3 collective-permute-start.2
  11.8 0.1 pad_add_fusion.refs_5_.me_ref
  11.9 5.8 %fetch.1 = (bf16[3584,1024]{1,0:T(8,128)(2,1)S(1)}, bf16[3584,1024]{1,0:T(8,128)(2,1)S(1)}, f32[8,3584]{1,0:T(8,128)S(1)}, f32[1,3584]{1,0:T(1,128)S(1)}) custom-call(bf16[3584,1024]{1,0:T(8,128)(2,1)} %bitcast.62, bf16[3584,1024]{1,0:T(8,128)(2,1)} %bitcast.63, f32[8,3584]{1,0:T(8,128)} %bitcast.67, f32[1,3584]{1,0:T(1,128)} %refs_3_.1, ...), custom_call_target="tpu_custom_call" | custom-call | bytes 14809088 | tf_op jit(solution)/shard_map/fetch/pallas_call | solution.py:77
  17.6 0.0 collective-permute-done.refs_1_
  17.7 0.0 collective-permute-done.6.refs_7_
  17.7 0.0 collective-permute-done.4.refs_5_
  17.7 0.0 collective-permute-done.2.refs_3_
  17.7 0.0 copy-start
  17.7 0.0 copy-start.1
  17.7 11.6 %experts.1 = (bf16[1,16,3584]{2,1,0:T(8,128)(2,1)S(1)}, bf16[1,16,3584]{2,1,0:T(8,128)(2,1)S(1)}, bf16[1,16,3584]{2,1,0:T(8,128)(2,1)S(1)}, bf16[1,16,3584]{2,1,...) custom-call(s32[3]{0:T(128)S(1)} %pad_add_fusion.refs_5_.me_ref, ...), custom_call_target="tpu_custom_call" | custom-call | tf_op jit(solution)/shard_map/experts/pallas_call | solution.py:215
  29.3 0.3 collective-permute-start.8
  29.6 0.3 collective-permute-start.7
  29.9 0.8 %collective-permute-done.8 = bf16[1,16,3584]{2,1,0:T(8,128)(2,1)S(1)} collective-permute-done((bf16[1,16,3584]{2,1,0:T(8,128)(2,1)S(1)}, bf16[1,16,3584]{2,1,0:T(8,128)(2,1)S(1)}, u32[]{:S(2)}, u32[]{:S(2)}) %collective-permute-start.8) | collective-permute-done | bytes 114720 | tf_op jit(solution)/shard_map/ppermute | solution.py:23
  30.7 1.9 %collective-permute-start.9 = (bf16[1,16,3584]{2,1,0:T(8,128)(2,1)S(1)}, bf16[1,16,3584]{2,1,0:T(8,128)(2,1)S(1)}, u32[]{:S(2)}, u32[]{:S(2)}) collective-permute-start(bf16[1,16,3584]{2,1,0:T(8,128)(2,1)S(1)} %add_convert_fusion), channel_id=1, source_target_pairs={{0,6},{1,7},{2,4},{3,5},{4,2},{5,3},{6,0},{7,1},{8,14},{9,15},{10,... | collective-permute-start | bytes 344072 | tf_op jit(solution)/shard_map/ppermute | solution.py:23
  32.6 0.0 collective-permute-done.7
  32.6 0.1 fusion.1
  32.7 1.4 %collective-permute-start.10 = (bf16[1,16,3584]{2,1,0:T(8,128)(2,1)S(1)}, bf16[1,16,3584]{2,1,0:T(8,128)(2,1)S(1)}, u32[]{:S(2)}, u32[]{:S(2)}) collective-permute-start(bf16[1,16,3584]{2,1,0:T(8,128)(2,1)S(1)} %get-tuple-element.40), channel_id=1, source_target_pairs={{0,2},{1,3},{2,0},{3,1},{4,6},{5,7},{6,4},{7,5},{8,10},{9,11},{10,... | collective-permute-start | bytes 344072 | tf_op jit(solution)/shard_map/ppermute | solution.py:23
  34.1 0.3 collective-permute-start.11
  34.4 3.3 %collective-permute-done.9 = bf16[1,16,3584]{2,1,0:T(8,128)(2,1)S(1)} collective-permute-done((bf16[1,16,3584]{2,1,0:T(8,128)(2,1)S(1)}, bf16[1,16,3584]{2,1,0:T(8,128)(2,1)S(1)}, u32[]{:S(2)}, u32[]{:S(2)}) %collective-permute-start.9) | collective-permute-done | bytes 114720 | tf_op jit(solution)/shard_map/ppermute | solution.py:23
  37.7 1.9 %collective-permute-done.10 = bf16[1,16,3584]{2,1,0:T(8,128)(2,1)S(1)} collective-permute-done((bf16[1,16,3584]{2,1,0:T(8,128)(2,1)S(1)}, bf16[1,16,3584]{2,1,0:T(8,128)(2,1)S(1)}, u32[]{:S(2)}, u32[]{:S(2)}) %collective-permute-start.10) | collective-permute-done | bytes 114720 | tf_op jit(solution)/shard_map/ppermute | solution.py:23
  39.6 0.0 collective-permute-done.11
  39.6 0.1 add_add_fusion
  39.7 0.0 copy-done
  39.7 0.0 copy-done.1
  39.7 0.7 %collective-permute-start.13 = (bf16[8,3584]{1,0:T(8,128)(2,1)S(1)}, bf16[8,3584]{1,0:T(8,128)(2,1)S(1)}, u32[]{:S(2)}, u32[]{:S(2)}) collective-permute-start(bf16[8,3584]{1,0:T(8,128)(2,1)S(1)} %get-tuple-element.38), channel_id=1, source_target_pairs={{1,9},{9,1},{3,11},{11,3},{5,13},{13,5},{7,15},{15,7},{8,16},{16,8... | collective-permute-start | bytes 172040 | tf_op jit(solution)/shard_map/ppermute | solution.py:298
  40.4 6.3 %collective-permute-start.12 = (bf16[8,3584]{1,0:T(8,128)(2,1)S(1)}, bf16[8,3584]{1,0:T(8,128)(2,1)S(1)}, u32[]{:S(2)}, u32[]{:S(2)}) collective-permute-start(bf16[8,3584]{1,0:T(8,128)(2,1)S(1)} %get-tuple-element.39), channel_id=1, source_target_pairs={{0,8},{8,0},{2,10},{10,2},{4,12},{12,4},{6,14},{14,6},{9,17},{17,9... | collective-permute-start | bytes 172040 | tf_op jit(solution)/shard_map/ppermute | solution.py:298
  46.7 0.0 collective-permute-done.13
  46.7 2.1 %collective-permute-done.12 = bf16[8,3584]{1,0:T(8,128)(2,1)S(1)} collective-permute-done((bf16[8,3584]{1,0:T(8,128)(2,1)S(1)}, bf16[8,3584]{1,0:T(8,128)(2,1)S(1)}, u32[]{:S(2)}, u32[]{:S(2)}) %collective-permute-start.12) | collective-permute-done | bytes 57376 | tf_op jit(solution)/shard_map/ppermute | solution.py:298
  48.9 0.7 %select_bitcast_fusion = (bf16[1,8,3584]{2,1,0:T(8,128)(2,1)}, bf16[1,8,3584]{2,1,0:T(8,128)(2,1)}) fusion(bf16[8,3584]{1,0:T(8,128)(2,1)S(1)} %collective-permute-done.13, bf16[8,3584]{1,0:T(8,128)(2,1)S(1)} %collective-permute-done.12, pred[]{:T(512)S(6)} %eq.3), kind=kLoop, calls=%fused_computation.17 | loop fusion | flops 57344 | bytes 229377 | tf_op jit(solution)/shard_map/broadcast_in_dim | solution.py:304
  (2 shorter events, 0.1 us)
Async XLA Ops:
  1.5 7.6 %collective-permute-start.5 = (bf16[1,16,3712]{2,1,0:T(8,128)(2,1)S(1)}, bf16[1,16,3712]{2,1,0:T(8,128)(2,1)S(1)}, u32[]{:S(2)}, u32[]{:S(2)}) collective-permute-start(bf16[1,16,3712]{2,1,0:T(8,128)(2,1)S(1)} %pack.1.refs_4_.refs_0_), channel_id=1, source_target_pairs={{0,6},{1,7},{2,4},{3,5},{4,2},{5,3},{6,0},{7,1},{8,14},{9,15},{10,... | collective-permute-start | bytes 356360 | tf_op jit(solution)/shard_map/ppermute | solution.py:23
  5.5 5.8 %collective-permute-start.3 = (bf16[1,16,3712]{2,1,0:T(8,128)(2,1)S(1)}, bf16[1,16,3712]{2,1,0:T(8,128)(2,1)S(1)}, u32[]{:S(2)}, u32[]{:S(2)}) collective-permute-start(bf16[1,16,3712]{2,1,0:T(8,128)(2,1)S(1)} %pack.1.refs_4_.refs_0_), channel_id=1, source_target_pairs={{0,4},{1,5},{2,6},{3,7},{4,0},{5,1},{6,2},{7,3},{8,12},{9,13},{10,... | collective-permute-start | bytes 356360 | tf_op jit(solution)/shard_map/ppermute | solution.py:23
  6.0 5.5 %collective-permute-start.1 = (bf16[1,16,3712]{2,1,0:T(8,128)(2,1)S(1)}, bf16[1,16,3712]{2,1,0:T(8,128)(2,1)S(1)}, u32[]{:S(2)}, u32[]{:S(2)}) collective-permute-start(bf16[1,16,3712]{2,1,0:T(8,128)(2,1)S(1)} %pack.1.refs_4_.refs_0_), channel_id=1, source_target_pairs={{0,2},{1,3},{2,0},{3,1},{4,6},{5,7},{6,4},{7,5},{8,10},{9,11},{10,... | collective-permute-start | bytes 356360 | tf_op jit(solution)/shard_map/ppermute | solution.py:23
  6.2 11.5 %collective-permute-start = (bf16[1,16,3712]{2,1,0:T(8,128)(2,1)S(1)}, bf16[1,16,3712]{2,1,0:T(8,128)(2,1)S(1)}, u32[]{:S(2)}, u32[]{:S(2)}) collective-permute-start(bf16[1,16,3712]{2,1,0:T(8,128)(2,1)S(1)} %pack.1.refs_4_.refs_0_), channel_id=1, source_target_pairs={{0,1},{1,0},{2,3},{3,2},{4,5},{5,4},{6,7},{7,6},{8,9},{9,8},{10,11... | collective-permute-start | bytes 356360 | tf_op jit(solution)/shard_map/ppermute | solution.py:23
  9.1 8.5 %collective-permute-start.6 = (bf16[1,16,3712]{2,1,0:T(8,128)(2,1)S(1)}, bf16[1,16,3712]{2,1,0:T(8,128)(2,1)S(1)}, u32[]{:S(2)}, u32[]{:S(2)}) collective-permute-start(bf16[1,16,3712]{2,1,0:T(8,128)(2,1)S(1)} %collective-permute-done.5.refs_6_), channel_id=1, source_target_pairs={{0,1},{1,0},{2,3},{3,2},{4,5},{5,4},{6,7},{7,6},{8,9},{9,8},{10,11... | collective-permute-start | bytes 356360 | tf_op jit(solution)/shard_map/ppermute | solution.py:23
  11.3 6.4 %collective-permute-start.4 = (bf16[1,16,3712]{2,1,0:T(8,128)(2,1)S(1)}, bf16[1,16,3712]{2,1,0:T(8,128)(2,1)S(1)}, u32[]{:S(2)}, u32[]{:S(2)}) collective-permute-start(bf16[1,16,3712]{2,1,0:T(8,128)(2,1)S(1)} %collective-permute-done.3.refs_4_), channel_id=1, source_target_pairs={{0,1},{1,0},{2,3},{3,2},{4,5},{5,4},{6,7},{7,6},{8,9},{9,8},{10,11... | collective-permute-start | bytes 356360 | tf_op jit(solution)/shard_map/ppermute | solution.py:23
  11.5 6.1 %collective-permute-start.2 = (bf16[1,16,3712]{2,1,0:T(8,128)(2,1)S(1)}, bf16[1,16,3712]{2,1,0:T(8,128)(2,1)S(1)}, u32[]{:S(2)}, u32[]{:S(2)}) collective-permute-start(bf16[1,16,3712]{2,1,0:T(8,128)(2,1)S(1)} %collective-permute-done.1.refs_2_), channel_id=1, source_target_pairs={{0,1},{1,0},{2,3},{3,2},{4,5},{5,4},{6,7},{7,6},{8,9},{9,8},{10,11... | collective-permute-start | bytes 356360 | tf_op jit(solution)/shard_map/ppermute | solution.py:23
  17.7 22.0 %copy-start = (bf16[1,8,3584]{2,1,0:T(8,128)(2,1)S(1)}, bf16[1,8,3584]{2,1,0:T(8,128)(2,1)}, u32[]{:S(2)}) copy-start(bf16[1,8,3584]{2,1,0:T(8,128)(2,1)} %param.8) | copy-start | bytes 172036
  17.7 22.0 %copy-start.1 = (bf16[1,8,3584]{2,1,0:T(8,128)(2,1)S(1)}, bf16[1,8,3584]{2,1,0:T(8,128)(2,1)}, u32[]{:S(2)}) copy-start(bf16[1,8,3584]{2,1,0:T(8,128)(2,1)} %param.9) | copy-start | bytes 172036
  29.3 1.4 %collective-permute-start.8 = (bf16[1,16,3584]{2,1,0:T(8,128)(2,1)S(1)}, bf16[1,16,3584]{2,1,0:T(8,128)(2,1)S(1)}, u32[]{:S(2)}, u32[]{:S(2)}) collective-permute-start(bf16[1,16,3584]{2,1,0:T(8,128)(2,1)S(1)} %get-tuple-element.35), channel_id=1, source_target_pairs={{0,1},{1,0},{2,3},{3,2},{4,5},{5,4},{6,7},{7,6},{8,9},{9,8},{10,11... | collective-permute-start | bytes 344072 | tf_op jit(solution)/shard_map/ppermute | solution.py:23
  29.6 3.0 %collective-permute-start.7 = (bf16[3,1,16,3584]{3,2,1,0:T(8,128)(2,1)S(1)}, bf16[3,1,16,3584]{3,2,1,0:T(8,128)(2,1)S(1)}, u32[]{:S(2)}, u32[]{:S(2)}) collective-permute-start(bf16[3,1,16,3584]{3,2,1,0:T(8,128)(2,1)S(1)} %get-tuple-element.33), channel_id=1, source_target_pairs={{0,1},{1,0},{2,3},{3,2},{4,5},{5,4},{6,7},{7,6},{8,9},{9,8},{10,11... | collective-permute-start | bytes 1032200 | tf_op jit(solution)/shard_map/ppermute | solution.py:23
  30.7 7.0 %collective-permute-start.9 = (bf16[1,16,3584]{2,1,0:T(8,128)(2,1)S(1)}, bf16[1,16,3584]{2,1,0:T(8,128)(2,1)S(1)}, u32[]{:S(2)}, u32[]{:S(2)}) collective-permute-start(bf16[1,16,3584]{2,1,0:T(8,128)(2,1)S(1)} %add_convert_fusion), channel_id=1, source_target_pairs={{0,6},{1,7},{2,4},{3,5},{4,2},{5,3},{6,0},{7,1},{8,14},{9,15},{10,... | collective-permute-start | bytes 344072 | tf_op jit(solution)/shard_map/ppermute | solution.py:23
  32.7 6.9 %collective-permute-start.10 = (bf16[1,16,3584]{2,1,0:T(8,128)(2,1)S(1)}, bf16[1,16,3584]{2,1,0:T(8,128)(2,1)S(1)}, u32[]{:S(2)}, u32[]{:S(2)}) collective-permute-start(bf16[1,16,3584]{2,1,0:T(8,128)(2,1)S(1)} %get-tuple-element.40), channel_id=1, source_target_pairs={{0,2},{1,3},{2,0},{3,1},{4,6},{5,7},{6,4},{7,5},{8,10},{9,11},{10,... | collective-permute-start | bytes 344072 | tf_op jit(solution)/shard_map/ppermute | solution.py:23
  34.1 5.5 %collective-permute-start.11 = (bf16[1,16,3584]{2,1,0:T(8,128)(2,1)S(1)}, bf16[1,16,3584]{2,1,0:T(8,128)(2,1)S(1)}, u32[]{:S(2)}, u32[]{:S(2)}) collective-permute-start(bf16[1,16,3584]{2,1,0:T(8,128)(2,1)S(1)} %get-tuple-element.41), channel_id=1, source_target_pairs={{0,4},{1,5},{2,6},{3,7},{4,0},{5,1},{6,2},{7,3},{8,12},{9,13},{10,... | collective-permute-start | bytes 344072 | tf_op jit(solution)/shard_map/ppermute | solution.py:23
  39.7 7.0 %collective-permute-start.13 = (bf16[8,3584]{1,0:T(8,128)(2,1)S(1)}, bf16[8,3584]{1,0:T(8,128)(2,1)S(1)}, u32[]{:S(2)}, u32[]{:S(2)}) collective-permute-start(bf16[8,3584]{1,0:T(8,128)(2,1)S(1)} %get-tuple-element.38), channel_id=1, source_target_pairs={{1,9},{9,1},{3,11},{11,3},{5,13},{13,5},{7,15},{15,7},{8,16},{16,8... | collective-permute-start | bytes 172040 | tf_op jit(solution)/shard_map/ppermute | solution.py:298
  40.4 8.5 %collective-permute-start.12 = (bf16[8,3584]{1,0:T(8,128)(2,1)S(1)}, bf16[8,3584]{1,0:T(8,128)(2,1)S(1)}, u32[]{:S(2)}, u32[]{:S(2)}) collective-permute-start(bf16[8,3584]{1,0:T(8,128)(2,1)S(1)} %get-tuple-element.39), channel_id=1, source_target_pairs={{0,8},{8,0},{2,10},{10,2},{4,12},{12,4},{6,14},{14,6},{9,17},{17,9... | collective-permute-start | bytes 172040 | tf_op jit(solution)/shard_map/ppermute | solution.py:298
